TPU v7x, 32 devices: a whole 2x2x4 slice. The times are simulated.
32 devices in a mesh: tiles: 2 (over y), disp: 4 (over z), rows: 2 (over x), cols: 2 (over core).
Axes of the slice: x: 2, y: 2, z: 4, core: 2. Of those that a mesh axis runs over, the one named last changes fastest.
Arguments:
- left_feat: bfloat16 [4, 256, 320], P(('tiles', 'rows'), ('cols', 'disp')), parts along dimension 0, may hold values from -64 to 64
- right_feat: bfloat16 [4, 256, 320], P(('tiles', 'rows'), ('cols', 'disp')), parts along dimension 0, may hold values from -64 to 64
- conv_first: bfloat16 [27, 32, 40], replicated, may hold values from -0.1875 to 0.1875
- conv_mid: bfloat16 [2, 27, 32, 32], replicated, may hold values from -0.21875 to 0.21875
- conv_last: bfloat16 [27, 1, 32], replicated, may hold values from -3 to 3
Outputs:
- estimate: float32 [4, 256], P(('tiles', 'rows'), ('cols', 'disp')), parts along dimension 0
There are 2 independent parts, one for each index of `tiles`. A program takes and returns all parts, laid end to end along the dimension named above; an argument that names none is the same for every part. Nothing has to cross between parts.
All inputs are finite; a program needn't handle non-finite values.
Results may differ from a plain program's by a relative error of at most 0.012.
The roundings to bfloat16 on the way count: a program that leaves them out, or rounds other values in their place, can miss the bound.
Values may be sent and summed in bfloat16 or wider, within the bound.
A program may use at most 64 MiB of HBM per device.

v0:
```python
import functools

import jax
import jax.numpy as jnp
import numpy as np
from jax import lax
from jax.experimental import pallas as pl
from jax.experimental.pallas import tpu as pltpu
from jax.sharding import PartitionSpec as P

MID = 2
DDEV = 16


def extended_2(block, sides, width):
    for axis, dim in sides:
        count = lax.axis_size(axis)
        forward = [(i, i + 1) for i in range(count - 1)]
        backward = [(target, source) for source, target in forward]
        low = lax.ppermute(
            lax.slice_in_dim(block, block.shape[dim] - width, None, axis=dim), axis, forward
        )
        high = lax.ppermute(lax.slice_in_dim(block, 0, width, axis=dim), axis, backward)
        block = jnp.concatenate([low, block, high], axis=dim)
    return block


def passed_along(x, axis, by):
    peers = lax.axis_size(axis)
    pairs = [(i, i + by) for i in range(peers) if 0 <= i + by < peers]
    return lax.ppermute(x, axis, pairs)


def combined_all(part, axis, combine):
    gathered = jax.tree.map(lambda a: lax.all_gather(a, axis), part)

    def take(source):
        return jax.tree.map(lambda a: lax.dynamic_index_in_dim(a, source, 0, False), gathered)

    return lax.fori_loop(
        1, lax.axis_size(axis), lambda source, state: combine(state, take(source)), take(0)
    )


def correlate(left_full, extended, groups, first_disp, count, total_disp):
    rows_here, width_here, channels = left_full.shape
    group_size = channels // groups
    left_groups = left_full.reshape(rows_here, width_here, groups, group_size)

    def single(offset):
        disp_value = first_disp + offset
        shifted = lax.dynamic_slice_in_dim(extended, 2 * width_here - disp_value, width_here, 1)
        right_groups = shifted.reshape(rows_here, width_here, groups, group_size)
        corr = (
            jnp.einsum(
                "hwgc,hwgc->ghw", left_groups, right_groups, preferred_element_type=jnp.float32
            )
            / group_size
        )
        inside = (disp_value >= 0) & (disp_value < total_disp)
        return jnp.where(inside, corr, 0.0).astype(jnp.bfloat16)

    return lax.map(single, jnp.arange(count, dtype=jnp.int32))


def convolve(padded, kernel):
    depth_out = padded.shape[0] - 2
    in_chans = padded.shape[1]
    rows_out = padded.shape[2] - 2
    cols_out = padded.shape[3] - 2
    out_chans = kernel.shape[1]
    columns = jnp.concatenate(
        [
            padded[:, :, row_tap : row_tap + rows_out, col_tap : col_tap + cols_out]
            for row_tap in range(3)
            for col_tap in range(3)
        ],
        axis=1,
    )
    flat = columns.reshape(depth_out + 2, 9 * in_chans, rows_out * cols_out)
    summed = jnp.zeros((depth_out, out_chans, rows_out * cols_out), jnp.float32)
    for disp_tap in range(3):
        taps = (
            jnp.transpose(kernel[9 * disp_tap : 9 * disp_tap + 9], (1, 0, 2))
            .reshape(out_chans, 9 * in_chans)
            .astype(flat.dtype)
        )
        summed = summed + jnp.einsum(
            "ok,dkn->don",
            taps,
            flat[disp_tap : disp_tap + depth_out],
            preferred_element_type=jnp.float32,
            precision=lax.Precision.HIGHEST,
        )
    return summed.reshape(depth_out, out_chans, rows_out, cols_out)


def widen(hidden):
    return extended_2(hidden, (("disp", 0), ("rows", 2), ("cols", 3)), 1)


def combine_parts(earlier, later):
    highest = jnp.maximum(earlier[0], later[0])
    scale_one = jnp.exp(earlier[0] - highest)
    scale_two = jnp.exp(later[0] - highest)
    return (
        highest,
        earlier[1] * scale_one + later[1] * scale_two,
        earlier[2] * scale_one + later[2] * scale_two,
    )


def shards(left_feat, right_feat, conv_first, conv_mid, conv_last):
    piece_width = left_feat.shape[1]
    groups = conv_first.shape[2]
    disp_count = lax.axis_size("disp")
    depth_here = DDEV
    total_disp = depth_here * disp_count
    first_disp = lax.axis_index("disp") * depth_here
    left_full, right_full = (
        lax.all_gather(left_feat, "disp", axis=1, tiled=True),
        lax.all_gather(right_feat, "disp", axis=1, tiled=True),
    )
    prior_full = passed_along(right_full, "cols", 1)
    extended = jnp.concatenate([jnp.zeros_like(right_full), prior_full, right_full], axis=1)
    volume = correlate(left_full, extended, groups, first_disp, depth_here, total_disp)
    padded = extended_2(volume, (("disp", 0), ("rows", 2), ("cols", 3)), 1)
    hidden = jax.nn.relu(convolve(padded, conv_first))
    for layer in range(MID):
        hidden = jax.nn.relu(convolve(widen(hidden), conv_mid[layer]))
    cost_cube = convolve(widen(hidden), conv_last)[:, 0]
    levels = (
        (first_disp + jnp.arange(depth_here, dtype=jnp.int32)).astype(jnp.float32) / total_disp
    )[:, None, None]
    local_high = jnp.max(cost_cube, axis=0)
    weights = jnp.exp(cost_cube - local_high[None])
    merged = combined_all(
        (local_high, jnp.sum(weights, axis=0), jnp.sum(weights * levels, axis=0)),
        "disp",
        combine_parts,
    )
    whole_row = merged[2] / merged[1]
    return lax.dynamic_slice_in_dim(whole_row, lax.axis_index("disp") * piece_width, piece_width, 1)


HALO = 4
GROUP = 4


def permutation(channels, groups):
    size = channels // groups
    out = np.zeros((2 * channels, size * 128), np.float32)
    for row in range(2):
        for c in range(channels):
            out[row * channels + c, (c % size) * 128 + row * 64 + c // size] = 1
    return out


def tap_choice():
    out = np.zeros((GROUP + 2, 2, GROUP, 2, 3, 3), np.float32)
    for d_in in range(GROUP + 2):
        for d_out in range(GROUP):
            for r_in in range(2):
                for r_out in range(2):
                    if 0 <= d_in - d_out <= 2:
                        out[d_in, r_in, d_out, r_out, d_in - d_out, r_in - r_out + 1] = 1
    return out


def banded(kernel):
    outs, ins = kernel.shape[1:]
    taps = kernel.reshape(3, 3, 3, outs, ins)
    choice = jnp.asarray(tap_choice(), jnp.bfloat16)
    return jnp.einsum(
        "drqsab,abeoi->drieqso", choice, taps, preferred_element_type=jnp.bfloat16
    )


def whole_kernel(
    disps, width_all, feat_ref, perm_ref, first_ref, mid_ref, last_ref, out_ref, a_ref, p_ref, f_ref
):
    width_here = out_ref.shape[1]
    wide = width_here + 2 * HALO
    span = disps + wide
    groups_d = disps // GROUP + 1
    rows = groups_d * wide
    f_ref[...] = jnp.dot(feat_ref[...], perm_ref[...], preferred_element_type=jnp.float32)
    a_ref[...] = jnp.zeros_like(a_ref)
    size = f_ref.shape[1] // 128
    for d in range(disps):
        acc = None
        for k in range(size):
            lanes = slice(128 * k, 128 * k + 128)
            start = wide + disps - d
            term = f_ref[0:wide, lanes] * f_ref[start : start + wide, lanes]
            acc = term if acc is None else acc + term
        slab = (acc / size).astype(jnp.bfloat16)
        stored = d + HALO
        group, place = divmod(stored, GROUP)
        a_ref[group * wide : (group + 1) * wide, 128 * place : 128 * place + 128] = slab
        if place < 2 and group > 0:
            lane = 128 * (GROUP + place)
            a_ref[(group - 1) * wide : group * wide, lane : lane + 128] = slab

    piece = lax.axis_index("cols") * lax.axis_size("disp") + lax.axis_index("disp")
    column = piece * width_here - HALO + lax.broadcasted_iota(jnp.int32, (wide, 256), 0)
    in_image = (column >= 0) & (column < width_all)
    lane_disp = lax.broadcasted_iota(jnp.int32, (wide, 256), 1) // 64

    for layer in range(MID + 1):
        taps_ref = first_ref if layer == 0 else mid_ref.at[layer - 1]
        if layer == 0:
            p_ref[8 : 8 + rows, :] = jnp.dot(
                a_ref[...], taps_ref[...], preferred_element_type=jnp.float32
            )
        else:
            taps = taps_ref[...]
            p_ref[8 : 8 + rows, :] = jnp.dot(
                a_ref[...],
                jnp.concatenate([taps, taps], axis=0),
                preferred_element_type=jnp.float32,
            )
        base = layer + 1 - HALO
        for group in range(groups_d):
            at = 8 + group * wide
            total = (
                p_ref[at - 1 : at - 1 + wide, 0:256]
                + p_ref[at : at + wide, 256:512]
                + p_ref[at + 1 : at + 1 + wide, 512:768]
            )
            low = base + GROUP * group
            keep = in_image
            if low < 0 or low + GROUP > disps:
                keep = keep & (lane_disp >= -low) & (lane_disp < disps - low)
            total = jnp.where(keep, jnp.maximum(total, 0.0), 0.0)
            high = total.astype(jnp.bfloat16)
            rest = (total - high.astype(jnp.float32)).astype(jnp.bfloat16)
            here = slice(group * wide, (group + 1) * wide)
            a_ref[here, 0:256] = high
            a_ref[here, 384:640] = rest
            if group > 0:
                before = slice((group - 1) * wide, group * wide)
                a_ref[before, 256:384] = high[:, 0:128]
                a_ref[before, 640:768] = rest[:, 0:128]
            if group == groups_d - 1:
                a_ref[here, 256:384] = jnp.zeros((wide, 128), jnp.bfloat16)
                a_ref[here, 640:768] = jnp.zeros((wide, 128), jnp.bfloat16)

    used = (groups_d - 1) * wide
    taps = last_ref[...]
    p_ref[8 : 8 + used, 0:384] = jnp.dot(
        a_ref[0:used], jnp.concatenate([taps, taps], axis=0), preferred_element_type=jnp.float32
    )
    costs = []
    for group in range(groups_d - 1):
        at = 8 + group * wide
        costs.append(
            p_ref[at - 1 : at - 1 + wide, 0:128]
            + p_ref[at : at + wide, 128:256]
            + p_ref[at + 1 : at + 1 + wide, 256:384]
        )
    lane = lax.broadcasted_iota(jnp.int32, (wide, 128), 1)
    mine = lane % 2 == lax.axis_index("rows")
    mine = mine & (lane < 2 * GROUP)
    top = functools.reduce(jnp.maximum, costs)
    top = jnp.max(jnp.where(mine, top, -jnp.inf), axis=1, keepdims=True)
    weight_sum = jnp.zeros((wide, 128), jnp.float32)
    level_sum = jnp.zeros((wide, 128), jnp.float32)
    for group, cost in enumerate(costs):
        weight = jnp.where(mine, jnp.exp(jnp.where(mine, cost - top, 0.0)), 0.0)
        level = (lane // 2 + GROUP * group).astype(jnp.float32) * (1.0 / disps)
        weight_sum += weight
        level_sum += weight * level
    estimate = jnp.sum(level_sum, axis=1, keepdims=True) / jnp.sum(
        weight_sum, axis=1, keepdims=True
    )
    place = lax.broadcasted_iota(jnp.int32, (wide, 128), 0)
    line = jnp.sum(jnp.where(place == lane + HALO, estimate, 0.0), axis=0, keepdims=True)
    out_ref[...] = line[:, 0:width_here]


def gathered_features(left_feat, right_feat, disps):
    width = left_feat.shape[1]
    both = jnp.concatenate([left_feat, right_feat], axis=0)
    other = lax.ppermute(both, "rows", [(0, 1), (1, 0)])
    first = lax.axis_index("rows") == 0
    pair = jnp.concatenate([jnp.where(first, both, other), jnp.where(first, other, both)], axis=2)
    peers = lax.axis_size("cols") * lax.axis_size("disp")

    def at(piece):
        col, disp = divmod(piece, lax.axis_size("disp"))
        return disp * lax.axis_size("cols") + col

    def moved(x, by):
        pairs = [(at(i), at(i + by)) for i in range(peers) if 0 <= i + by < peers]
        return lax.ppermute(x, ("disp", "cols"), pairs)

    left, right = pair[0], pair[1]
    after = moved(pair[:, :HALO], -1)
    before_left = moved(left[width - HALO :], 1)
    before = []
    needed = disps + HALO
    by = 1
    while needed > 0:
        take = min(width, needed)
        before.insert(0, moved(right[width - take :], by))
        needed -= take
        by += 1
    return jnp.concatenate(
        [before_left, left, after[0]] + before + [right, after[1]], axis=0
    )


def window_shards(left_feat, right_feat, conv_first, conv_mid, conv_last):
    width = left_feat.shape[1]
    channels = left_feat.shape[2]
    groups = conv_first.shape[2]
    disps = DDEV * lax.axis_size("disp")
    width_all = width * lax.axis_size("disp") * lax.axis_size("cols")
    feats = gathered_features(left_feat, right_feat, disps)
    perm = jnp.asarray(permutation(channels, groups), jnp.bfloat16)
    first = banded(jnp.pad(conv_first, ((0, 0), (0, 0), (0, 64 - groups)))).reshape(768, 768)
    mid = jax.vmap(banded)(conv_mid).reshape(MID, 384, 768)
    last = banded(conv_last).reshape(384, 3, 8)
    last = jnp.pad(last, ((0, 0), (0, 0), (0, 120))).reshape(384, 384)
    wide = width + 2 * HALO
    rows = (disps // GROUP + 1) * wide
    return pl.pallas_call(
        functools.partial(whole_kernel, disps, width_all),
        out_shape=jax.ShapeDtypeStruct((1, width), jnp.float32),
        in_specs=[pl.BlockSpec(memory_space=pltpu.VMEM)] * 5,
        out_specs=pl.BlockSpec(memory_space=pltpu.VMEM),
        scratch_shapes=[
            pltpu.VMEM((rows, 768), jnp.bfloat16),
            pltpu.VMEM((rows + 16, 768), jnp.float32),
            pltpu.VMEM((2 * wide + disps, (channels // groups) * 128), jnp.float32),
        ],
        compiler_params=pltpu.CompilerParams(vmem_limit_bytes=48 * 1024 * 1024),
    )(feats, perm, first, mid, last)


def solution(mesh):
    rows, pieces = mesh.shape["rows"], mesh.shape["cols"] * mesh.shape["disp"]
    body = window_shards if rows == 2 and pieces == 8 else shards
    return jax.shard_map(
        body,
        mesh=mesh,
        in_specs=(
            P(("tiles", "rows"), ("cols", "disp"), None),
            P(("tiles", "rows"), ("cols", "disp"), None),
            P(),
            P(),
            P(),
        ),
        out_specs=P(("tiles", "rows"), ("cols", "disp")),
        check_vma=False,
    )
```

profile of v0, /device:TPU:0, one launch (start us, length us, event | category | flops | bytes accessed | tf_op | source)
XLA Modules:
  0.0 82.6 jit_solution(11793438513112654242)
XLA Ops:
  0.0 0.8 constant_dynamic-update-slice_fusion.1
  0.8 0.7 constant_dynamic-update-slice_fusion
  1.5 2.9 %collective-permute-start = (bf16[2,32,320]{2,1,0:T(8,128)(2,1)S(1)}, bf16[2,32,320]{2,1,0:T(8,128)(2,1)S(1)}, u32[]{:S(2)}, u32[]{:S(2)}) collective-permute-start(bf16[2,32,320]{2,1,0:T(8,128)(2,1)S(1)} %constant_dynamic-update-slice_fusion), channel_id=1, source_target_pairs={{0,2},{2,0},{1,3},{3,1},{4,6},{6,4},{5,7},{7,5},{8,10},{10,8},{9,1... | collective-permute-start | bytes 122888 | tf_op jit(solution)/shard_map/ppermute | solution.py:285
  4.5 0.7 reshape.30
  5.2 5.3 %convolution_bitcast_fusion = bf16[2,6,2,32,3,4,2,32]{3,1,7,4,0,6,5,2:T(8,128)(2,1)} fusion(bf16[6,2,4,2,3,3,1,1,1]{0,5,4,8,7,6,3,2,1:T(4,128)(2,1)} %constant.21, bf16[2,3,3,3,32,32,1,1,1]{5,4,3,2,1,0,8,7,6:T(8,128)(2,1)S(1)} %bitcast.57), kind=kOutput, calls=%fused_computation | convolution fusion | flops 10616832 | bytes 1291968 | tf_op jit(solution)/shard_map/vmap(drqsab,abeoi->drieqso)/dot_general | solution.py:174
  10.6 0.2 convolution_bitcast_fusion.2
  10.8 2.8 %convolution_bitcast_fusion.1 = bf16[6,2,64,3,4,2,32]{2,0,5,4,1,6,3:T(8,128)(2,1)} fusion(bf16[6,2,4,2,3,3,1,1]{0,5,4,3,2,1,7,6:T(4,128)(2,1)S(1)} %copy-done.3, bf16[3,3,3,32,64,1,1,1]{4,3,2,1,0,7,6,5:T(8,128)(2,1)S(1)} %bitcast.58), kind=kOutput, calls=%fused_computation.1 | convolution fusion | flops 10616832 | bytes 1291968 | tf_op jit(solution)/shard_map/drqsab,abeoi->drieqso/dot_general | solution.py:174
  13.7 12.7 %copy.17 = bf16[2,6,2,32,3,4,2,32]{7,6,5,4,3,2,1,0:T(2,128)(2,1)} copy(bf16[2,6,2,32,3,4,2,32]{3,1,7,4,0,6,5,2:T(8,128)(2,1)} %convolution_bitcast_fusion) | data formatting | bytes 2359296 | tf_op jit(solution)/shard_map/vmap(drqsab,abeoi->drieqso)/transpose | solution.py:174
  26.4 12.2 %reshape.29.mid_ref = bf16[2,384,768]{2,1,0:T(8,128)(2,1)S(1)} reshape(bf16[2,6,2,32,3,4,2,32]{7,6,5,4,3,2,1,0:T(2,128)(2,1)} %copy.17) | data formatting | bytes 2359296 | tf_op jit(solution)/shard_map/reshape | solution.py:323
  38.6 7.0 %copy.15 = bf16[6,2,64,3,4,2,32]{2,1,0,6,5,4,3:T(2,128)(2,1)} copy(bf16[6,2,64,3,4,2,32]{2,0,5,4,1,6,3:T(8,128)(2,1)} %convolution_bitcast_fusion.1) | data formatting | bytes 2359296 | tf_op jit(solution)/shard_map/drqsab,abeoi->drieqso/transpose | solution.py:174
  45.5 5.6 %reshape.27 = bf16[768,768]{0,1:T(8,128)(2,1)} reshape(bf16[6,2,64,3,4,2,32]{2,1,0,6,5,4,3:T(2,128)(2,1)} %copy.15) | data formatting | bytes 2359296 | tf_op jit(solution)/shard_map/reshape | solution.py:322
  51.1 1.6 %copy.20.first_ref = bf16[768,768]{1,0:T(8,128)(2,1)S(1)} copy(bf16[768,768]{0,1:T(8,128)(2,1)} %reshape.27) | data formatting | bytes 2359296 | tf_op jit(solution)/shard_map/reshape | solution.py:322
  52.8 0.1 reshape.31
  52.9 0.2 copy.21.last_ref
  53.2 0.1 fusion.4
  53.2 4.5 %collective-permute-start.4 = (bf16[32,640]{1,0:T(8,128)(2,1)S(1)}, bf16[32,640]{1,0:T(8,128)(2,1)S(1)}, u32[]{:S(2)}, u32[]{:S(2)}) collective-permute-start(bf16[32,640]{1,0:T(8,128)(2,1)S(1)} %get-tuple-element.5), channel_id=1, source_target_pairs={{0,8},{4,12},{8,1},{12,5},{1,9},{5,13},{2,10},{6,14},{10,3},{14,7}... | collective-permute-start | bytes 122888 | tf_op jit(solution)/shard_map/ppermute | solution.py:296
  57.8 3.5 %collective-permute-start.5 = (bf16[32,640]{1,0:T(8,128)(2,1)S(1)}, bf16[32,640]{1,0:T(8,128)(2,1)S(1)}, u32[]{:S(2)}, u32[]{:S(2)}) collective-permute-start(bf16[32,640]{1,0:T(8,128)(2,1)S(1)} %get-tuple-element.5), channel_id=1, source_target_pairs={{0,4},{4,8},{8,12},{12,1},{1,5},{5,9},{9,13},{2,6},{6,10},{10,14},... | collective-permute-start | bytes 122888 | tf_op jit(solution)/shard_map/ppermute | solution.py:296
  61.3 1.3 %collective-permute-start.2 = (bf16[2,4,640]{2,1,0:T(4,128)(2,1)S(1)}, bf16[2,4,640]{2,1,0:T(4,128)(2,1)S(1)}, u32[]{:S(2)}, u32[]{:S(2)}) collective-permute-start(bf16[2,4,640]{2,1,0:T(4,128)(2,1)S(1)} %fusion.5), channel_id=1, source_target_pairs={{4,0},{8,4},{12,8},{1,12},{5,1},{9,5},{13,9},{6,2},{10,6},{14,10},... | collective-permute-start | bytes 30728 | tf_op jit(solution)/shard_map/ppermute | solution.py:296
  62.7 4.5 %collective-permute-start.1 = (bf16[4,640]{1,0:T(4,128)(2,1)S(1)}, bf16[4,640]{1,0:T(4,128)(2,1)S(1)}, u32[]{:S(2)}, u32[]{:S(2)}) collective-permute-start(bf16[4,640]{1,0:T(4,128)(2,1)S(1)} %get-tuple-element.8), channel_id=1, source_target_pairs={{0,4},{4,8},{8,12},{12,1},{1,5},{5,9},{9,13},{2,6},{6,10},{10,14},... | collective-permute-start | bytes 15368 | tf_op jit(solution)/shard_map/ppermute | solution.py:296
  67.2 4.7 %collective-permute-start.3 = (bf16[4,640]{1,0:T(4,128)(2,1)S(1)}, bf16[4,640]{1,0:T(4,128)(2,1)S(1)}, u32[]{:S(2)}, u32[]{:S(2)}) collective-permute-start(bf16[4,640]{1,0:T(4,128)(2,1)S(1)} %get-tuple-element.7), channel_id=1, source_target_pairs={{0,12},{4,1},{8,5},{12,9},{1,13},{2,14},{6,3},{10,7},{14,11},{3,15... | collective-permute-start | bytes 15368 | tf_op jit(solution)/shard_map/ppermute | solution.py:296
  72.0 1.1 %collective-permute-done.3 = bf16[4,640]{1,0:T(4,128)(2,1)S(1)} collective-permute-done((bf16[4,640]{1,0:T(4,128)(2,1)S(1)}, bf16[4,640]{1,0:T(4,128)(2,1)S(1)}, u32[]{:S(2)}, u32[]{:S(2)}) %collective-permute-start.3) | collective-permute-done | bytes 5152 | tf_op jit(solution)/shard_map/ppermute | solution.py:296
  73.1 0.9 %concatenate.11.feat_ref = bf16[144,640]{1,0:T(8,128)(2,1)S(1)} concatenate(bf16[4,640]{1,0:T(4,128)(2,1)S(1)} %collective-permute-done.1, bf16[32,640]{1,0:T(8,128)(2,1)S(1)} %get-tuple-element.6, bf16[4,640]{1,0:T(4,128)(2,1)S(1)} %get-tuple-element.12, bf16[4,640]{1,0:T(4,128)(2,1)S(1)} %collective-permute-done.3, bf16[32,640]{1,0:T(8,128)(2,1)S(1)} %collective-permute-done.4, ...), dimensions={0} | concatenate | bytes 368640 | tf_op jit(solution)/shard_map/concatenate | solution.py:309
  74.1 1.3 %copy-done.1 = bf16[640,1024]{1,0:T(8,128)(2,1)S(1)} copy-done((bf16[640,1024]{1,0:T(8,128)(2,1)S(1)}, bf16[640,1024]{1,0:T(8,128)(2,1)}, u32[]{:S(2)}) %copy-start.1) | copy-done | bytes 1310744
  75.4 7.2 %shard_map.91 = f32[1,32]{1,0:T(1,128)} custom-call(bf16[144,640]{1,0:T(8,128)(2,1)S(1)} %concatenate.11.feat_ref, bf16[640,1024]{1,0:T(8,128)(2,1)S(1)} %copy-done.1, bf16[768,768]{1,0:T(8,128)(2,1)S(1)} %copy.20.first_ref, bf16[2,384,768]{2,1,0:T(8,128)(2,1)S(1)} %reshape.29.mid_ref, bf16[384,384]{1,0:T(8,128)(2,1)S(1)} %copy.21.last_ref), custom_call_target="tpu_custom_call" | custom-call | tf_op jit(solution)/shard_map/pallas_call | solution.py:328
  (21 shorter events, 0.4 us)
Async XLA Ops:
  0.0 5.2 %copy-start = (bf16[2,27,32,32]{3,2,1,0:T(8,128)(2,1)S(1)}, bf16[2,27,32,32]{3,2,1,0:T(8,128)(2,1)}, u32[]{:S(2)}) copy-start(bf16[2,27,32,32]{3,2,1,0:T(8,128)(2,1)} %param.12) | copy-start | bytes 331780
  1.5 51.6 %collective-permute-start = (bf16[2,32,320]{2,1,0:T(8,128)(2,1)S(1)}, bf16[2,32,320]{2,1,0:T(8,128)(2,1)S(1)}, u32[]{:S(2)}, u32[]{:S(2)}) collective-permute-start(bf16[2,32,320]{2,1,0:T(8,128)(2,1)S(1)} %constant_dynamic-update-slice_fusion), channel_id=1, source_target_pairs={{0,2},{2,0},{1,3},{3,1},{4,6},{6,4},{5,7},{7,5},{8,10},{10,8},{9,1... | collective-permute-start | bytes 122888 | tf_op jit(solution)/shard_map/ppermute | solution.py:285
  5.2 5.3 %copy-start.2 = (bf16[27,32,40]{2,1,0:T(8,128)(2,1)S(1)}, bf16[27,32,40]{2,1,0:T(8,128)(2,1)}, u32[]{:S(2)}) copy-start(bf16[27,32,40]{2,1,0:T(8,128)(2,1)} %param.11) | copy-start | bytes 207364
  5.2 5.4 %copy-start.4 = (bf16[6,2,4,2,3,3,1]{0,5,4,6,3,2,1:T(4,128)(2,1)S(1)}, bf16[6,2,4,2,3,3,1]{0,5,4,6,3,2,1:T(4,128)(2,1)}, u32[]{:S(2)}) copy-start(bf16[6,2,4,2,3,3,1]{0,5,4,6,3,2,1:T(4,128)(2,1)} %constant.22) | copy-start | bytes 5188
  5.2 5.6 %copy-start.3 = (bf16[6,2,4,2,3,3,1,1]{0,5,4,3,2,1,7,6:T(4,128)(2,1)S(1)}, bf16[6,2,4,2,3,3,1,1]{0,5,4,3,2,1,7,6:T(4,128)(2,1)}, u32[]{:S(2)}) copy-start(bf16[6,2,4,2,3,3,1,1]{0,5,4,3,2,1,7,6:T(4,128)(2,1)} %constant.20) | copy-start | bytes 5188
  53.2 19.9 %collective-permute-start.4 = (bf16[32,640]{1,0:T(8,128)(2,1)S(1)}, bf16[32,640]{1,0:T(8,128)(2,1)S(1)}, u32[]{:S(2)}, u32[]{:S(2)}) collective-permute-start(bf16[32,640]{1,0:T(8,128)(2,1)S(1)} %get-tuple-element.5), channel_id=1, source_target_pairs={{0,8},{4,12},{8,1},{12,5},{1,9},{5,13},{2,10},{6,14},{10,3},{14,7}... | collective-permute-start | bytes 122888 | tf_op jit(solution)/shard_map/ppermute | solution.py:296
  57.8 15.4 %collective-permute-start.5 = (bf16[32,640]{1,0:T(8,128)(2,1)S(1)}, bf16[32,640]{1,0:T(8,128)(2,1)S(1)}, u32[]{:S(2)}, u32[]{:S(2)}) collective-permute-start(bf16[32,640]{1,0:T(8,128)(2,1)S(1)} %get-tuple-element.5), channel_id=1, source_target_pairs={{0,4},{4,8},{8,12},{12,1},{1,5},{5,9},{9,13},{2,6},{6,10},{10,14},... | collective-permute-start | bytes 122888 | tf_op jit(solution)/shard_map/ppermute | solution.py:296
  61.3 10.7 %collective-permute-start.2 = (bf16[2,4,640]{2,1,0:T(4,128)(2,1)S(1)}, bf16[2,4,640]{2,1,0:T(4,128)(2,1)S(1)}, u32[]{:S(2)}, u32[]{:S(2)}) collective-permute-start(bf16[2,4,640]{2,1,0:T(4,128)(2,1)S(1)} %fusion.5), channel_id=1, source_target_pairs={{4,0},{8,4},{12,8},{1,12},{5,1},{9,5},{13,9},{6,2},{10,6},{14,10},... | collective-permute-start | bytes 30728 | tf_op jit(solution)/shard_map/ppermute | solution.py:296
  62.7 9.3 %collective-permute-start.1 = (bf16[4,640]{1,0:T(4,128)(2,1)S(1)}, bf16[4,640]{1,0:T(4,128)(2,1)S(1)}, u32[]{:S(2)}, u32[]{:S(2)}) collective-permute-start(bf16[4,640]{1,0:T(4,128)(2,1)S(1)} %get-tuple-element.8), channel_id=1, source_target_pairs={{0,4},{4,8},{8,12},{12,1},{1,5},{5,9},{9,13},{2,6},{6,10},{10,14},... | collective-permute-start | bytes 15368 | tf_op jit(solution)/shard_map/ppermute | solution.py:296
  67.2 5.9 %collective-permute-start.3 = (bf16[4,640]{1,0:T(4,128)(2,1)S(1)}, bf16[4,640]{1,0:T(4,128)(2,1)S(1)}, u32[]{:S(2)}, u32[]{:S(2)}) collective-permute-start(bf16[4,640]{1,0:T(4,128)(2,1)S(1)} %get-tuple-element.7), channel_id=1, source_target_pairs={{0,12},{4,1},{8,5},{12,9},{1,13},{2,14},{6,3},{10,7},{14,11},{3,15... | collective-permute-start | bytes 15368 | tf_op jit(solution)/shard_map/ppermute | solution.py:296
  74.0 1.3 %copy-start.1 = (bf16[640,1024]{1,0:T(8,128)(2,1)S(1)}, bf16[640,1024]{1,0:T(8,128)(2,1)}, u32[]{:S(2)}) copy-start(bf16[640,1024]{1,0:T(8,128)(2,1)} %constant.12.clone.perm_ref) | copy-start | bytes 3932164
where the time goes:
time: 83.4 us; the launch traced here: 82.6 us
  local copies, waits for them, and re-layouts  44 us (53%)
  starting transfers between devices  21.5 us (26%)
  matrix products  8.34 us (10%)
  Pallas kernels  7.21 us (9%)
  waiting for transfers between devices  1.12 us (1%)
    transpose x3, local copies, waits for them, and re-layouts, banded(): jnp.einsum('drqsab,abeoi->drieqso', choice, taps, preferred_element_type=...  19.8 us
    ppermute x5, starting transfers between devices, moved(): return lax.ppermute(x, ('disp', 'cols'), pairs)  18.5 us
    reshape x1, local copies, waits for them, and re-layouts, window_shards(): mid = jax.vmap(banded)(conv_mid).reshape(MID, 384, 768)  12.2 us
    dot_general x3, matrix products, banded(): jnp.einsum('drqsab,abeoi->drieqso', choice, taps, preferred_element_type=...  8.34 us
    pallas_call x1, Pallas kernels, window_shards(): pl.pallas_call(functools.partial(whole_kernel, disps, width_all), out_sha...  7.21 us
    reshape x2, local copies, waits for them, and re-layouts, window_shards(): banded(jnp.pad(conv_first, ((0, 0), (0, 0), (0, 64 - groups))))  7.14 us
    ppermute x1, starting transfers between devices, gathered_features(): other = lax.ppermute(both, 'rows', [(0, 1), (1, 0)])  2.94 us
    unnamed x11, local copies, waits for them, and re-layouts  2.13 us
  transfers between devices with their start and end apart: 6, of which 1 were waited for; matrix products, arithmetic and copies ran while one was open for 59% of the time, Pallas kernels for 0%

commit v1 on v0

--- a/solution.py
+++ b/solution.py
@@ -2,7 +2,6 @@
 
 import jax
 import jax.numpy as jnp
-import numpy as np
 from jax import lax
 from jax.experimental import pallas as pl
 from jax.experimental.pallas import tpu as pltpu
@@ -147,52 +146,128 @@
 GROUP = 4
 
 
-def permutation(channels, groups):
+EDGE = 16
+
+
+def permutation(row, channels, groups):
     size = channels // groups
-    out = np.zeros((2 * channels, size * 128), np.float32)
-    for row in range(2):
-        for c in range(channels):
-            out[row * channels + c, (c % size) * 128 + row * 64 + c // size] = 1
-    return out
-
-
-def tap_choice():
-    out = np.zeros((GROUP + 2, 2, GROUP, 2, 3, 3), np.float32)
-    for d_in in range(GROUP + 2):
+    lane = lax.broadcasted_iota(jnp.int32, (1, 128 * size), 1)
+    group = lane % 64
+    wanted = group * size + lane // 128
+    wanted = jnp.where((group < groups) & ((lane // 64) % 2 == row), wanted, -1)
+    channel = lax.broadcasted_iota(jnp.int32, (channels, 128 * size), 0)
+    return (channel == wanted).astype(jnp.float32).astype(jnp.bfloat16)
+
+
+def tap_of(a, r_in, r_out, e):
+    return 9 * a + 3 * (r_in - r_out + 1) + e
+
+
+def build_first(taps_ref, banded_ref):
+    banded_ref[...] = jnp.zeros_like(banded_ref)
+    outs, ins = taps_ref.shape[1:]
+    blank = jnp.zeros((outs, 64 - ins), jnp.float32)
+    for e in range(3):
+        for r_out in range(2):
+            for a in range(3):
+                slabs = []
+                for r_in in range(2):
+                    slabs += [taps_ref[tap_of(a, r_in, r_out, e)].astype(jnp.float32), blank]
+                block = jnp.concatenate(slabs, axis=1).astype(jnp.bfloat16)
+                for d_out in range(GROUP):
+                    at = e * 256 + d_out * 64 + r_out * 32
+                    lane = 128 * (d_out + a)
+                    banded_ref[at : at + outs, lane : lane + 128] = block
+
+
+def build_mid(taps_ref, banded_ref):
+    banded_ref[...] = jnp.zeros_like(banded_ref)
+    outs = taps_ref.shape[1]
+    blank = jnp.zeros((outs, 64), jnp.float32)
+    for e in range(3):
+        for r_out in range(2):
+            slabs = [
+                taps_ref[tap_of(a, r_in, r_out, e)].astype(jnp.float32)
+                for a in range(3)
+                for r_in in range(2)
+            ]
+            even = jnp.concatenate(slabs + [blank], axis=1).astype(jnp.bfloat16)
+            odd = jnp.concatenate([blank] + slabs, axis=1).astype(jnp.bfloat16)
+            for d_out in range(GROUP):
+                at = e * 256 + d_out * 64 + r_out * 32
+                block = even if d_out % 2 == 0 else odd
+                for lane in (128 * (d_out // 2), 384 + 128 * (d_out // 2)):
+                    banded_ref[at : at + outs, lane : lane + 256] = block
+
+
+def build_last(taps_ref, banded_ref):
+    banded_ref[...] = jnp.zeros_like(banded_ref)
+    for e in range(3):
+        lines = []
         for d_out in range(GROUP):
-            for r_in in range(2):
-                for r_out in range(2):
-                    if 0 <= d_in - d_out <= 2:
-                        out[d_in, r_in, d_out, r_out, d_in - d_out, r_in - r_out + 1] = 1
-    return out
-
-
-def banded(kernel):
-    outs, ins = kernel.shape[1:]
-    taps = kernel.reshape(3, 3, 3, outs, ins)
-    choice = jnp.asarray(tap_choice(), jnp.bfloat16)
-    return jnp.einsum(
-        "drqsab,abeoi->drieqso", choice, taps, preferred_element_type=jnp.bfloat16
+            for r_out in range(2):
+                parts = [
+                    taps_ref[tap_of(a, r_in, r_out, e)].astype(jnp.float32)
+                    for a in range(3)
+                    for r_in in range(2)
+                ]
+                if d_out > 0:
+                    parts.insert(0, jnp.zeros((1, 64 * d_out), jnp.float32))
+                if d_out < GROUP - 1:
+                    parts.append(jnp.zeros((1, 64 * (GROUP - 1 - d_out)), jnp.float32))
+                lines.append(jnp.concatenate(parts, axis=1))
+        lines.append(jnp.zeros((8, 384), jnp.float32))
+        block = jnp.concatenate(lines, axis=0).astype(jnp.bfloat16)
+        banded_ref[128 * e : 128 * e + 16, 0:384] = block
+        banded_ref[128 * e : 128 * e + 16, 384:768] = block
+
+
+def across(x, banded):
+    return lax.dot_general(
+        x, banded, (((1,), (1,)), ((), ())), preferred_element_type=jnp.float32
     )
 
 
 def whole_kernel(
-    disps, width_all, feat_ref, perm_ref, first_ref, mid_ref, last_ref, out_ref, a_ref, p_ref, f_ref
+    disps,
+    width_all,
+    feat_ref,
+    first_taps,
+    mid_taps,
+    last_taps,
+    out_ref,
+    a_ref,
+    p_ref,
+    f_ref,
+    first_ref,
+    mid_ref,
+    last_ref,
 ):
     width_here = out_ref.shape[1]
     wide = width_here + 2 * HALO
     span = disps + wide
     groups_d = disps // GROUP + 1
     rows = groups_d * wide
-    f_ref[...] = jnp.dot(feat_ref[...], perm_ref[...], preferred_element_type=jnp.float32)
+    build_first(first_taps, first_ref)
+    for layer in range(MID):
+        build_mid(mid_taps.at[layer], mid_ref.at[layer])
+    build_last(last_taps, last_ref)
+    channels, groups = feat_ref.shape[2], first_taps.shape[2]
+    f_ref[...] = jnp.dot(
+        feat_ref[0], permutation(0, channels, groups), preferred_element_type=jnp.float32
+    ) + jnp.dot(
+        feat_ref[1], permutation(1, channels, groups), preferred_element_type=jnp.float32
+    )
+    left_at = EDGE - HALO
+    right_at = width_here + 2 * EDGE + EDGE - HALO
     a_ref[...] = jnp.zeros_like(a_ref)
     size = f_ref.shape[1] // 128
     for d in range(disps):
         acc = None
         for k in range(size):
             lanes = slice(128 * k, 128 * k + 128)
-            start = wide + disps - d
-            term = f_ref[0:wide, lanes] * f_ref[start : start + wide, lanes]
+            start = right_at + disps - d
+            term = f_ref[left_at : left_at + wide, lanes] * f_ref[start : start + wide, lanes]
             acc = term if acc is None else acc + term
         slab = (acc / size).astype(jnp.bfloat16)
         stored = d + HALO
@@ -209,17 +284,7 @@
 
     for layer in range(MID + 1):
         taps_ref = first_ref if layer == 0 else mid_ref.at[layer - 1]
-        if layer == 0:
-            p_ref[8 : 8 + rows, :] = jnp.dot(
-                a_ref[...], taps_ref[...], preferred_element_type=jnp.float32
-            )
-        else:
-            taps = taps_ref[...]
-            p_ref[8 : 8 + rows, :] = jnp.dot(
-                a_ref[...],
-                jnp.concatenate([taps, taps], axis=0),
-                preferred_element_type=jnp.float32,
-            )
+        p_ref[8 : 8 + rows, :] = across(a_ref[...], taps_ref[...])
         base = layer + 1 - HALO
         for group in range(groups_d):
             at = 8 + group * wide
@@ -247,10 +312,7 @@
                 a_ref[here, 640:768] = jnp.zeros((wide, 128), jnp.bfloat16)
 
     used = (groups_d - 1) * wide
-    taps = last_ref[...]
-    p_ref[8 : 8 + used, 0:384] = jnp.dot(
-        a_ref[0:used], jnp.concatenate([taps, taps], axis=0), preferred_element_type=jnp.float32
-    )
+    p_ref[8 : 8 + used, 0:384] = across(a_ref[0:used], last_ref[...])
     costs = []
     for group in range(groups_d - 1):
         at = 8 + group * wide
@@ -279,36 +341,106 @@
     out_ref[...] = line[:, 0:width_here]
 
 
-def gathered_features(left_feat, right_feat, disps):
-    width = left_feat.shape[1]
-    both = jnp.concatenate([left_feat, right_feat], axis=0)
-    other = lax.ppermute(both, "rows", [(0, 1), (1, 0)])
-    first = lax.axis_index("rows") == 0
-    pair = jnp.concatenate([jnp.where(first, both, other), jnp.where(first, other, both)], axis=2)
-    peers = lax.axis_size("cols") * lax.axis_size("disp")
-
-    def at(piece):
-        col, disp = divmod(piece, lax.axis_size("disp"))
-        return disp * lax.axis_size("cols") + col
-
-    def moved(x, by):
-        pairs = [(at(i), at(i + by)) for i in range(peers) if 0 <= i + by < peers]
-        return lax.ppermute(x, ("disp", "cols"), pairs)
-
-    left, right = pair[0], pair[1]
-    after = moved(pair[:, :HALO], -1)
-    before_left = moved(left[width - HALO :], 1)
-    before = []
-    needed = disps + HALO
-    by = 1
-    while needed > 0:
-        take = min(width, needed)
-        before.insert(0, moved(right[width - take :], by))
-        needed -= take
-        by += 1
-    return jnp.concatenate(
-        [before_left, left, after[0]] + before + [right, after[1]], axis=0
-    )
+def exchange_kernel(copies, left_ref, right_ref, out_ref, held, send_sem, recv_sem):
+    width = left_ref.shape[1]
+    row, col, disp = lax.axis_index("rows"), lax.axis_index("cols"), lax.axis_index("disp")
+    col_disps = lax.axis_size("disp")
+    pieces = col_disps * lax.axis_size("cols")
+    piece = col * col_disps + disp
+    held[...] = jnp.zeros_like(held)
+
+    def device(other, by):
+        target = piece + by
+        return {
+            "tiles": lax.axis_index("tiles"),
+            "disp": target % col_disps,
+            "rows": (row + other) % 2,
+            "cols": target // col_disps,
+        }
+
+    def exists(by):
+        return (piece + by >= 0) & (piece + by < pieces)
+
+    barrier = pltpu.get_barrier_semaphore()
+    partners = jnp.int32(0)
+    for by in range(-3, 4):
+        for other in range(2):
+            if by == 0 and other == 0:
+                continue
+
+            @pl.when(exists(by))
+            def _():
+                pl.semaphore_signal(
+                    barrier,
+                    inc=1,
+                    device_id=device(other, by),
+                    device_id_type=pl.DeviceIdType.MESH,
+                )
+
+            partners = partners + exists(by).astype(jnp.int32)
+    pl.semaphore_wait(barrier, partners)
+
+    def copy(number):
+        view, by, other, source, target, count = copies[number]
+        return pltpu.make_async_remote_copy(
+            src_ref=(left_ref if view == 0 else right_ref).at[0, pl.ds(source, count)],
+            dst_ref=held.at[row, pl.ds(target, count)],
+            send_sem=send_sem.at[number],
+            recv_sem=recv_sem.at[number],
+            device_id=device(other, by),
+            device_id_type=pl.DeviceIdType.MESH,
+        )
+
+    for number in range(len(copies)):
+
+        @pl.when(exists(copies[number][1]))
+        def _():
+            copy(number).start()
+
+    held[row, EDGE : EDGE + width] = left_ref[0]
+    own = width + 3 * EDGE + 2 * width
+    held[row, own : own + width] = right_ref[0]
+    for number in range(len(copies)):
+        by = copies[number][1]
+
+        @pl.when(exists(by))
+        def _():
+            copy(number).wait_send()
+
+        @pl.when(exists(-by))
+        def _():
+            copy(number).wait_recv()
+
+    out_ref[...] = held[...]
+
+
+def exchanged(left_feat, right_feat):
+    width, channels = left_feat.shape[1:]
+    right_at = width + 2 * EDGE
+    own = right_at + EDGE + 2 * width
+    copies = []
+    for other in (1, 0):
+        copies.append((1, 2, other, 0, own - 2 * width, width))
+        copies.append((1, 3, other, width - EDGE, right_at, EDGE))
+        copies.append((1, 1, other, 0, own - width, width))
+        copies.append((1, -1, other, 0, own + width, EDGE))
+        copies.append((0, 1, other, width - EDGE, 0, EDGE))
+        copies.append((0, -1, other, 0, EDGE + width, EDGE))
+    copies.append((1, 0, 1, 0, own, width))
+    copies.append((0, 0, 1, 0, EDGE, width))
+    shape = (2, own + width + EDGE, channels)
+    return pl.pallas_call(
+        functools.partial(exchange_kernel, tuple(copies)),
+        out_shape=jax.ShapeDtypeStruct(shape, jnp.bfloat16),
+        in_specs=[pl.BlockSpec(memory_space=pltpu.VMEM)] * 2,
+        out_specs=pl.BlockSpec(memory_space=pltpu.VMEM),
+        scratch_shapes=[
+            pltpu.VMEM(shape, jnp.bfloat16),
+            pltpu.SemaphoreType.DMA((len(copies),)),
+            pltpu.SemaphoreType.DMA((len(copies),)),
+        ],
+        compiler_params=pltpu.CompilerParams(collective_id=0, has_side_effects=True),
+    )(left_feat, right_feat)
 
 
 def window_shards(left_feat, right_feat, conv_first, conv_mid, conv_last):
@@ -317,31 +449,29 @@
     groups = conv_first.shape[2]
     disps = DDEV * lax.axis_size("disp")
     width_all = width * lax.axis_size("disp") * lax.axis_size("cols")
-    feats = gathered_features(left_feat, right_feat, disps)
-    perm = jnp.asarray(permutation(channels, groups), jnp.bfloat16)
-    first = banded(jnp.pad(conv_first, ((0, 0), (0, 0), (0, 64 - groups)))).reshape(768, 768)
-    mid = jax.vmap(banded)(conv_mid).reshape(MID, 384, 768)
-    last = banded(conv_last).reshape(384, 3, 8)
-    last = jnp.pad(last, ((0, 0), (0, 0), (0, 120))).reshape(384, 384)
+    feats = exchanged(left_feat, right_feat)
     wide = width + 2 * HALO
     rows = (disps // GROUP + 1) * wide
     return pl.pallas_call(
         functools.partial(whole_kernel, disps, width_all),
         out_shape=jax.ShapeDtypeStruct((1, width), jnp.float32),
-        in_specs=[pl.BlockSpec(memory_space=pltpu.VMEM)] * 5,
+        in_specs=[pl.BlockSpec(memory_space=pltpu.VMEM)] * 4,
         out_specs=pl.BlockSpec(memory_space=pltpu.VMEM),
         scratch_shapes=[
             pltpu.VMEM((rows, 768), jnp.bfloat16),
             pltpu.VMEM((rows + 16, 768), jnp.float32),
-            pltpu.VMEM((2 * wide + disps, (channels // groups) * 128), jnp.float32),
+            pltpu.VMEM((feats.shape[1], (channels // groups) * 128), jnp.float32),
+            pltpu.VMEM((768, 768), jnp.bfloat16),
+            pltpu.VMEM((MID, 768, 768), jnp.bfloat16),
+            pltpu.VMEM((384, 768), jnp.bfloat16),
         ],
         compiler_params=pltpu.CompilerParams(vmem_limit_bytes=48 * 1024 * 1024),
-    )(feats, perm, first, mid, last)
+    )(feats, conv_first, conv_mid, conv_last)
 
 
 def solution(mesh):
     rows, pieces = mesh.shape["rows"], mesh.shape["cols"] * mesh.shape["disp"]
-    body = window_shards if rows == 2 and pieces == 8 else shards
+    body = window_shards if rows == 2 and mesh.shape["disp"] == 4 and pieces == 8 else shards
     return jax.shard_map(
         body,
         mesh=mesh,

time: 83.4 us -> 23 us (0.28)
  local copies, waits for them, and re-layouts: 44 us -> 2.72 us
  starting transfers between devices: 21.5 us -> 0 us
  Pallas kernels: 7.21 us -> 20 us
  matrix products: 8.34 us -> 0 us
  waiting for transfers between devices: 1.12 us -> 0 us
    ppermute x6 -> x0, starting transfers between devices: 21.5 us -> none  [the longest x5 18.5 us: moved(): return lax.ppermute(x, ('disp', 'cols'), pairs)]
    transpose x3 -> x0, local copies, waits for them, and re-layouts: 19.8 us -> none  [banded(): jnp.einsum('drqsab,abeoi->drieqso', choice, taps, preferred_element_type=...]
    reshape x5 -> x0, local copies, waits for them, and re-layouts: 19.6 us -> none  [the longest x1 12.2 us: window_shards(): mid = jax.vmap(banded)(conv_mid).reshape(MID, 384, 768)]
    pallas_call x0 -> x1, Pallas kernels: none -> 11.9 us  [exchanged(): pl.pallas_call(functools.partial(exchange_kernel, tuple(copies)), out_sha...]
    dot_general x3 -> x0, matrix products: 8.34 us -> none  [banded(): jnp.einsum('drqsab,abeoi->drieqso', choice, taps, preferred_element_type=...]
    concatenate x2 -> x0, local copies, waits for them, and re-layouts: 1.67 us -> none  [the longest x1 0.93 us: gathered_features(): jnp.concatenate([before_left, left, after[0]] + before + [right, after[1]...]
    ppermute x6 -> x0, waiting for transfers between devices: 1.12 us -> none  [the longest x5 1.11 us: moved(): return lax.ppermute(x, ('disp', 'cols'), pairs)]
    pallas_call x1, Pallas kernels: 7.21 us -> 8.05 us  [window_shards(): pl.pallas_call(functools.partial(whole_kernel, disps, width_all), out_sha...]
  transfers between devices with their start and end apart: 6 -> 0, of which waited for: 1 -> 0; matrix products, arithmetic and copies ran while one was open for 59% -> 0% of each run, Pallas kernels for 0% -> 0%
where the time goes in v1:
time: 23 us; the launch traced here: 22.7 us
  Pallas kernels  20 us (87%)
  local copies, waits for them, and re-layouts  2.72 us (12%)
    pallas_call x1, Pallas kernels, exchanged(): pl.pallas_call(functools.partial(exchange_kernel, tuple(copies)), out_sha...  11.9 us
    pallas_call x1, Pallas kernels, window_shards(): pl.pallas_call(functools.partial(whole_kernel, disps, width_all), out_sha...  8.05 us
    unnamed x7, local copies, waits for them, and re-layouts  2.72 us

profile of v1, /device:TPU:0, one launch (start us, length us, event | category | flops | bytes accessed | tf_op | source)
XLA Modules:
  0.0 22.7 jit_solution(14861742327445118297)
XLA Ops:
  0.0 0.0 copy-start.2
  0.0 0.7 %copy.6.last_taps = bf16[27,1,32]{2,1,0:T(2,128)(2,1)S(1)} copy(bf16[27,1,32]{2,0,1:T(8,128)(2,1)} %param.9) | data formatting | bytes 3456 | tf_op args[4]
  0.8 11.9 %shard_map.55.feat_ref = bf16[2,192,320]{2,1,0:T(8,128)(2,1)} custom-call(bf16[1,32,320]{2,1,0:T(8,128)(2,1)} %left_ref.1, bf16[1,32,320]{2,1,0:T(8,128)(2,1)} %right_ref.1), custom_call_target="tpu_custom_call" | custom-call | tf_op jit(solution)/shard_map/pallas_call | solution.py:432
  12.7 0.0 copy-done.2
  12.7 0.0 copy-start
  12.7 1.0 %copy-done = bf16[2,192,320]{2,1,0:T(8,128)(2,1)S(1)} copy-done((bf16[2,192,320]{2,1,0:T(8,128)(2,1)S(1)}, bf16[2,192,320]{2,1,0:T(8,128)(2,1)}, u32[]{:S(2)}) %copy-start) | copy-done | bytes 245784
  13.7 0.0 copy-start.1
  13.7 1.0 %copy-done.1 = bf16[2,27,32,32]{3,2,1,0:T(8,128)(2,1)S(1)} copy-done((bf16[2,27,32,32]{3,2,1,0:T(8,128)(2,1)S(1)}, bf16[2,27,32,32]{3,2,1,0:T(8,128)(2,1)}, u32[]{:S(2)}) %copy-start.1) | copy-done | bytes 110616
  14.7 8.1 %shard_map.56 = f32[1,32]{1,0:T(1,128)} custom-call(bf16[2,192,320]{2,1,0:T(8,128)(2,1)S(1)} %copy-done, bf16[27,32,40]{2,1,0:T(8,128)(2,1)S(1)} %copy-done.2, bf16[2,27,32,32]{3,2,1,0:T(8,128)(2,1)S(1)} %copy-done.1, bf16[27,1,32]{2,1,0:T(2,128)(2,1)S(1)} %copy.6.last_taps), custom_call_target="tpu_custom_call" | custom-call | tf_op jit(solution)/shard_map/pallas_call | solution.py:455
Async XLA Ops:
  0.0 12.7 %copy-start.2 = (bf16[27,32,40]{2,1,0:T(8,128)(2,1)S(1)}, bf16[27,32,40]{2,1,0:T(8,128)(2,1)}, u32[]{:S(2)}) copy-start(bf16[27,32,40]{2,1,0:T(8,128)(2,1)} %first_taps.1) | copy-start | bytes 207364
  12.7 1.0 %copy-start = (bf16[2,192,320]{2,1,0:T(8,128)(2,1)S(1)}, bf16[2,192,320]{2,1,0:T(8,128)(2,1)}, u32[]{:S(2)}) copy-start(bf16[2,192,320]{2,1,0:T(8,128)(2,1)} %shard_map.55.feat_ref) | copy-start | bytes 737284
  13.7 1.0 %copy-start.1 = (bf16[2,27,32,32]{3,2,1,0:T(8,128)(2,1)S(1)}, bf16[2,27,32,32]{3,2,1,0:T(8,128)(2,1)}, u32[]{:S(2)}) copy-start(bf16[2,27,32,32]{3,2,1,0:T(8,128)(2,1)} %mid_taps.1) | copy-start | bytes 331780

commit v2 on v1

--- a/solution.py
+++ b/solution.py
@@ -202,12 +202,13 @@
 
 def build_last(taps_ref, banded_ref):
     banded_ref[...] = jnp.zeros_like(banded_ref)
+    taps = taps_ref[...].astype(jnp.float32)
     for e in range(3):
         lines = []
         for d_out in range(GROUP):
             for r_out in range(2):
                 parts = [
-                    taps_ref[tap_of(a, r_in, r_out, e)].astype(jnp.float32)
+                    taps[tap_of(a, r_in, r_out, e) : tap_of(a, r_in, r_out, e) + 1]
                     for a in range(3)
                     for r_in in range(2)
                 ]
@@ -228,14 +229,125 @@
     )
 
 
+def exchange_plan(width):
+    right_at = width + 2 * EDGE
+    own = right_at + EDGE + 2 * width
+    copies = []
+    for other in (1, 0):
+        copies.append((1, 2, other, 0, own - 2 * width, width))
+        copies.append((1, 3, other, width - EDGE, right_at, EDGE))
+        copies.append((1, 1, other, 0, own - width, width))
+        copies.append((1, -1, other, 0, own + width, EDGE))
+        copies.append((0, 1, other, width - EDGE, 0, EDGE))
+        copies.append((0, -1, other, 0, EDGE + width, EDGE))
+    copies.append((1, 0, 1, 0, own, width))
+    copies.append((0, 0, 1, 0, EDGE, width))
+    return tuple(copies), own, own + width + EDGE
+
+
+def exchange_steps(left_ref, right_ref, held, send_sem, recv_sem, own_sem):
+    width = left_ref.shape[1]
+    copies, own, _ = exchange_plan(width)
+    row, col, disp = lax.axis_index("rows"), lax.axis_index("cols"), lax.axis_index("disp")
+    col_disps = lax.axis_size("disp")
+    pieces = col_disps * lax.axis_size("cols")
+    piece = col * col_disps + disp
+    barrier = pltpu.get_barrier_semaphore()
+
+    def device(other, by):
+        target = piece + by
+        return {
+            "tiles": lax.axis_index("tiles"),
+            "disp": target % col_disps,
+            "rows": (row + other) % 2,
+            "cols": target // col_disps,
+        }
+
+    def exists(by):
+        return (piece + by >= 0) & (piece + by < pieces)
+
+    def copy(number):
+        view, by, other, source, target, count = copies[number]
+        return pltpu.make_async_remote_copy(
+            src_ref=(left_ref if view == 0 else right_ref).at[0, pl.ds(source, count)],
+            dst_ref=held.at[row, pl.ds(target, count)],
+            send_sem=send_sem.at[number],
+            recv_sem=recv_sem.at[number],
+            device_id=device(other, by),
+            device_id_type=pl.DeviceIdType.MESH,
+        )
+
+    def greet():
+        held[...] = jnp.zeros_like(held)
+        for by in range(-3, 4):
+            for other in range(2):
+                if by == 0 and other == 0:
+                    continue
+
+                @pl.when(exists(by))
+                def _():
+                    pl.semaphore_signal(
+                        barrier,
+                        inc=1,
+                        device_id=device(other, by),
+                        device_id_type=pl.DeviceIdType.MESH,
+                    )
+
+    def send():
+        partners = jnp.int32(-1)
+        for by in range(-3, 4):
+            partners = partners + 2 * exists(by).astype(jnp.int32)
+        pl.semaphore_wait(barrier, partners)
+        for number in range(len(copies)):
+
+            @pl.when(exists(copies[number][1]))
+            def _():
+                copy(number).start()
+
+        for load in own_loads:
+            load.start()
+
+    own_loads = [
+        pltpu.make_async_copy(
+            source.at[0], held.at[row, pl.ds(target, width)], own_sem.at[number]
+        )
+        for number, (source, target) in enumerate(((left_ref, EDGE), (right_ref, own)))
+    ]
+
+    def receive():
+        for load in own_loads:
+            load.wait()
+        for number in range(len(copies)):
+            by = copies[number][1]
+
+            @pl.when(exists(by))
+            def _():
+                copy(number).wait_send()
+
+            @pl.when(exists(-by))
+            def _():
+                copy(number).wait_recv()
+
+    return greet, send, receive
+
+
 def whole_kernel(
     disps,
     width_all,
+    left_ref,
+    right_ref,
+    first_hbm,
+    mid_hbm,
+    last_hbm,
+    out_ref,
     feat_ref,
+    send_sem,
+    recv_sem,
+    own_sem,
+    load_sem,
     first_taps,
     mid_taps,
     last_taps,
-    out_ref,
     a_ref,
     p_ref,
     f_ref,
@@ -248,10 +360,26 @@
     span = disps + wide
     groups_d = disps // GROUP + 1
     rows = groups_d * wide
+    greet, send, receive = exchange_steps(left_ref, right_ref, feat_ref, send_sem, recv_sem, own_sem)
+    loads = [
+        pltpu.make_async_copy(source, target, load_sem.at[number])
+        for number, (source, target) in enumerate(
+            ((first_hbm, first_taps), (mid_hbm, mid_taps), (last_hbm, last_taps))
+        )
+    ]
+    greet()
+    for load in loads:
+        load.start()
+    a_ref[...] = jnp.zeros_like(a_ref)
+    send()
+    loads[0].wait()
     build_first(first_taps, first_ref)
+    loads[1].wait()
     for layer in range(MID):
         build_mid(mid_taps.at[layer], mid_ref.at[layer])
+    loads[2].wait()
     build_last(last_taps, last_ref)
+    receive()
     channels, groups = feat_ref.shape[2], first_taps.shape[2]
     f_ref[...] = jnp.dot(
         feat_ref[0], permutation(0, channels, groups), preferred_element_type=jnp.float32
@@ -260,7 +388,6 @@
     )
     left_at = EDGE - HALO
     right_at = width_here + 2 * EDGE + EDGE - HALO
-    a_ref[...] = jnp.zeros_like(a_ref)
     size = f_ref.shape[1] // 128
     for d in range(disps):
         acc = None
@@ -341,132 +468,40 @@
     out_ref[...] = line[:, 0:width_here]
 
 
-def exchange_kernel(copies, left_ref, right_ref, out_ref, held, send_sem, recv_sem):
-    width = left_ref.shape[1]
-    row, col, disp = lax.axis_index("rows"), lax.axis_index("cols"), lax.axis_index("disp")
-    col_disps = lax.axis_size("disp")
-    pieces = col_disps * lax.axis_size("cols")
-    piece = col * col_disps + disp
-    held[...] = jnp.zeros_like(held)
-
-    def device(other, by):
-        target = piece + by
-        return {
-            "tiles": lax.axis_index("tiles"),
-            "disp": target % col_disps,
-            "rows": (row + other) % 2,
-            "cols": target // col_disps,
-        }
-
-    def exists(by):
-        return (piece + by >= 0) & (piece + by < pieces)
-
-    barrier = pltpu.get_barrier_semaphore()
-    partners = jnp.int32(0)
-    for by in range(-3, 4):
-        for other in range(2):
-            if by == 0 and other == 0:
-                continue
-
-            @pl.when(exists(by))
-            def _():
-                pl.semaphore_signal(
-                    barrier,
-                    inc=1,
-                    device_id=device(other, by),
-                    device_id_type=pl.DeviceIdType.MESH,
-                )
-
-            partners = partners + exists(by).astype(jnp.int32)
-    pl.semaphore_wait(barrier, partners)
-
-    def copy(number):
-        view, by, other, source, target, count = copies[number]
-        return pltpu.make_async_remote_copy(
-            src_ref=(left_ref if view == 0 else right_ref).at[0, pl.ds(source, count)],
-            dst_ref=held.at[row, pl.ds(target, count)],
-            send_sem=send_sem.at[number],
-            recv_sem=recv_sem.at[number],
-            device_id=device(other, by),
-            device_id_type=pl.DeviceIdType.MESH,
-        )
-
-    for number in range(len(copies)):
-
-        @pl.when(exists(copies[number][1]))
-        def _():
-            copy(number).start()
-
-    held[row, EDGE : EDGE + width] = left_ref[0]
-    own = width + 3 * EDGE + 2 * width
-    held[row, own : own + width] = right_ref[0]
-    for number in range(len(copies)):
-        by = copies[number][1]
-
-        @pl.when(exists(by))
-        def _():
-            copy(number).wait_send()
-
-        @pl.when(exists(-by))
-        def _():
-            copy(number).wait_recv()
-
-    out_ref[...] = held[...]
-
-
-def exchanged(left_feat, right_feat):
-    width, channels = left_feat.shape[1:]
-    right_at = width + 2 * EDGE
-    own = right_at + EDGE + 2 * width
-    copies = []
-    for other in (1, 0):
-        copies.append((1, 2, other, 0, own - 2 * width, width))
-        copies.append((1, 3, other, width - EDGE, right_at, EDGE))
-        copies.append((1, 1, other, 0, own - width, width))
-        copies.append((1, -1, other, 0, own + width, EDGE))
-        copies.append((0, 1, other, width - EDGE, 0, EDGE))
-        copies.append((0, -1, other, 0, EDGE + width, EDGE))
-    copies.append((1, 0, 1, 0, own, width))
-    copies.append((0, 0, 1, 0, EDGE, width))
-    shape = (2, own + width + EDGE, channels)
-    return pl.pallas_call(
-        functools.partial(exchange_kernel, tuple(copies)),
-        out_shape=jax.ShapeDtypeStruct(shape, jnp.bfloat16),
-        in_specs=[pl.BlockSpec(memory_space=pltpu.VMEM)] * 2,
-        out_specs=pl.BlockSpec(memory_space=pltpu.VMEM),
-        scratch_shapes=[
-            pltpu.VMEM(shape, jnp.bfloat16),
-            pltpu.SemaphoreType.DMA((len(copies),)),
-            pltpu.SemaphoreType.DMA((len(copies),)),
-        ],
-        compiler_params=pltpu.CompilerParams(collective_id=0, has_side_effects=True),
-    )(left_feat, right_feat)
-
-
 def window_shards(left_feat, right_feat, conv_first, conv_mid, conv_last):
     width = left_feat.shape[1]
     channels = left_feat.shape[2]
     groups = conv_first.shape[2]
     disps = DDEV * lax.axis_size("disp")
     width_all = width * lax.axis_size("disp") * lax.axis_size("cols")
-    feats = exchanged(left_feat, right_feat)
+    copies, _, held_rows = exchange_plan(width)
     wide = width + 2 * HALO
     rows = (disps // GROUP + 1) * wide
     return pl.pallas_call(
         functools.partial(whole_kernel, disps, width_all),
         out_shape=jax.ShapeDtypeStruct((1, width), jnp.float32),
-        in_specs=[pl.BlockSpec(memory_space=pltpu.VMEM)] * 4,
+        in_specs=[pl.BlockSpec(memory_space=pltpu.HBM)] * 5,
         out_specs=pl.BlockSpec(memory_space=pltpu.VMEM),
         scratch_shapes=[
+            pltpu.VMEM((2, held_rows, channels), jnp.bfloat16),
+            pltpu.SemaphoreType.DMA((len(copies),)),
+            pltpu.SemaphoreType.DMA((len(copies),)),
+            pltpu.SemaphoreType.DMA((2,)),
+            pltpu.SemaphoreType.DMA((3,)),
+            pltpu.VMEM(conv_first.shape, jnp.bfloat16),
+            pltpu.VMEM(conv_mid.shape, jnp.bfloat16),
+            pltpu.VMEM((27, conv_last.shape[2]), jnp.bfloat16),
             pltpu.VMEM((rows, 768), jnp.bfloat16),
             pltpu.VMEM((rows + 16, 768), jnp.float32),
-            pltpu.VMEM((feats.shape[1], (channels // groups) * 128), jnp.float32),
+            pltpu.VMEM((held_rows, (channels // groups) * 128), jnp.float32),
             pltpu.VMEM((768, 768), jnp.bfloat16),
             pltpu.VMEM((MID, 768, 768), jnp.bfloat16),
             pltpu.VMEM((384, 768), jnp.bfloat16),
         ],
-        compiler_params=pltpu.CompilerParams(vmem_limit_bytes=48 * 1024 * 1024),
-    )(feats, conv_first, conv_mid, conv_last)
+        compiler_params=pltpu.CompilerParams(
+            vmem_limit_bytes=56 * 1024 * 1024, collective_id=0, has_side_effects=True
+        ),
+    )(left_feat, right_feat, conv_first, conv_mid, conv_last.reshape(27, -1))
 
 
 def solution(mesh):

time: 23 us -> 20.1 us (0.87)
  local copies, waits for them, and re-layouts: 2.72 us -> 1.19 us
  Pallas kernels: 20 us -> 18.7 us
    pallas_call x1 -> x0, Pallas kernels: 11.9 us -> none  [exchanged(): pl.pallas_call(functools.partial(exchange_kernel, tuple(copies)), out_sha...]
    pallas_call x1, Pallas kernels: 8.05 us -> 18.7 us  [window_shards(): pl.pallas_call(functools.partial(whole_kernel, disps, width_all), out_sha...]
    unnamed x7 -> x1, local copies, waits for them, and re-layouts: 2.72 us -> 1.19 us
where the time goes in v2:
time: 20.1 us; the launch traced here: 19.9 us
  Pallas kernels  18.7 us (93%)
  local copies, waits for them, and re-layouts  1.19 us (6%)
    pallas_call x1, Pallas kernels, window_shards(): pl.pallas_call(functools.partial(whole_kernel, disps, width_all), out_sha...  18.7 us
    unnamed x1, local copies, waits for them, and re-layouts  1.19 us

profile of v2, /device:TPU:0, one launch (start us, length us, event | category | flops | bytes accessed | tf_op | source)
XLA Modules:
  0.0 19.9 jit_solution(66673145636690696)
XLA Ops:
  0.0 18.7 %shard_map.55 = f32[1,32]{1,0:T(1,128)} custom-call(bf16[1,32,320]{2,1,0:T(8,128)(2,1)} %left_ref.1, bf16[1,32,320]{2,1,0:T(8,128)(2,1)} %right_ref.1, bf16[27,32,40]{2,1,0:T(8,128)(2,1)} %first_hbm.1, bf16[2,27,32,32]{3,2,1,0:T(8,128)(2,1)} %mid_hbm.1, bf16[27,32]{1,0:T(8,128)(2,1)} %bitcast.1), custom_call_target="tpu_custom_call" | custom-call | tf_op jit(solution)/shard_map/pallas_call | solution.py:480
  18.7 1.2 %copy.7 = f32[1,32]{1,0:T(1,128)} copy(f32[1,32]{1,0:T(1,128)} %shard_map.55) | data formatting | bytes 256
